TPU v7x, 32 devices: a whole 2x2x4 slice. The times are simulated.
32 devices in a mesh: row: 8 (over y, x, core), col: 4 (over z).
Axes of the slice: x: 2, y: 2, z: 4, core: 2. Of those that a mesh axis runs over, the one named last changes fastest.
Arguments:
- a_blocks: bfloat16 [256, 12, 4096], P('row', 'col'), may hold values from -0.75 to 0.75
- columns: int32 [256, 12], P('row', 'col'), may hold values from 0 to 255, as said below
- prolong: bfloat16 [256, 4096], P(('row', 'col')), may hold values from -1.5 to 1.5
- partner: int32 [256], P('row'), may hold values from 0 to 31, as said below
Outputs:
- coarse: bfloat16 [128, 12, 4096], P('row', 'col')
Inputs may be any that keep to these rules, and one draw needn't show every extreme that they name: `columns`: entry k of a fine block row in row group g reaches a fine block row of group g - 1, g or g + 1 inside the grid, whose position within its group lies in [j * 8, (j + 1) * 8) with j = k // 3. Rows of groups 2q and 2q+1 are matched one to one: partner of a row in one group gives its partner's position in the other, and the two entries point at each other.
All inputs are finite; a program needn't handle non-finite values.
Results may differ from a plain program's by a relative error of at most 0.0058.
Values may be sent and summed in bfloat16 or wider, within the bound.
A program may use at most 64 MiB of HBM per device.

v0:
```python
import functools
import math

import jax
import jax.numpy as jnp
from jax import lax
from jax.experimental import pallas as pl
from jax.experimental.pallas import tpu as pltpu
from jax.sharding import PartitionSpec as P

MESH = pl.DeviceIdType.MESH
BF = jnp.bfloat16
F32 = jnp.float32
LANES = 128
CHUNK = 8


def iota(shape, dim):
    return lax.broadcasted_iota(jnp.int32, shape, dim)


def onehot(mask):
    return jnp.where(mask, 1.0, 0.0).astype(BF)


def kernel(dims, partner_hbm, cols_hbm, p_hbm, a_hbm, out_ref, partner_v, order_v, order, cols, p_ref, a_v, own_v, halo_v, af, hf, of, pf, bd, lv, wv, send_v, recv_v,
           partner_sem, order_sem, cols_sem, p_sem, a_sem, row_send, row_recv, col_send, col_recv, pair_send, pair_recv):
    nrow, ncol, rows, slots, thin, size, bs = dims
    tiles = size // LANES
    half = rows // 2
    chunks = half // CHUNK
    g = lax.axis_index("row")
    z = lax.axis_index("col")
    up = lax.rem(g + 1, nrow)
    down = lax.rem(g + nrow - 1, nrow)
    pair = g + 1 - 2 * lax.rem(g, 2)

    partner_copy = pltpu.make_async_copy(partner_hbm, partner_v, partner_sem)
    partner_copy.start()
    cols_copy = pltpu.make_async_copy(cols_hbm, cols, cols_sem)
    cols_copy.start()
    local = pltpu.make_async_copy(p_hbm, p_ref, p_sem)
    local.start()
    fetch = pltpu.make_async_copy(a_hbm, a_v, a_sem)
    fetch.start()

    barrier = pltpu.get_barrier_semaphore()
    for other in (up, down):
        pl.semaphore_signal(barrier, inc=1, device_id={"row": other}, device_id_type=MESH)
    for d in range(1, ncol):
        pl.semaphore_signal(barrier, inc=1, device_id={"col": lax.rem(z + d, ncol)}, device_id_type=MESH)
    pl.semaphore_wait(barrier, ncol + 1)

    row_copies = []
    for n, (other, slot) in enumerate(((up, 0), (down, 1))):
        copy = pltpu.make_async_remote_copy(
            src_ref=p_hbm, dst_ref=halo_v.at[slot], send_sem=row_send.at[n], recv_sem=row_recv.at[n],
            device_id={"row": other}, device_id_type=MESH)
        copy.start()
        row_copies.append(copy)
    col_copies = []
    for d in range(1, ncol):
        copy = pltpu.make_async_remote_copy(
            src_ref=p_hbm, dst_ref=own_v.at[d], send_sem=col_send.at[d], recv_sem=col_recv.at[d],
            device_id={"col": lax.rem(z + d, ncol)}, device_id_type=MESH)
        copy.start()
        col_copies.append(copy)

    def spread(source, target, base):
        for t in range(tiles):
            target[pl.ds(base + t * thin, thin), :] = source[:, t * LANES:(t + 1) * LANES].astype(F32)

    low = iota((tiles, LANES), 1) < bs
    r2, c2 = iota((2 * bs, 2 * bs), 0), iota((2 * bs, 2 * bs), 1)
    rh, ch = r2 // bs, c2 // bs
    rm, cm = r2 - rh * bs, c2 - ch * bs
    cs = cm // tiles
    weave = onehot((rh == ch) & (2 * (cm - cs * tiles) + cs == rm))
    r1, c1 = iota((bs, LANES), 0), iota((bs, LANES), 1)
    s1 = r1 // tiles
    pick = onehot(c1 == 2 * (r1 - s1 * tiles) + s1)

    def diagonals(slot):
        base = slot * tiles * thin
        for r in range(thin):
            packed = hf[pl.ds(base + r, tiles, stride=thin), :]
            turned = pltpu.roll(packed, bs, 1)
            zero = jnp.zeros_like(packed)
            stacked = jnp.concatenate(
                [jnp.where(low, packed, zero), jnp.where(low, turned, zero),
                 jnp.where(low, zero, turned), jnp.where(low, zero, packed)], axis=0).astype(BF)
            bd[slot * thin + r] = jnp.dot(weave, stacked, preferred_element_type=F32).astype(BF)

    partner_copy.wait()
    place = iota((rows, rows), 0)
    entry = iota((rows, rows), 1)
    position = jnp.where(lax.rem(g, 2) == 1, jnp.broadcast_to(partner_v[...], (rows, rows)),
                         jnp.where(entry < half, entry + half, entry - half))
    picked = jnp.sum(jnp.where(position == place, entry, 0).astype(F32), axis=1, keepdims=True)
    order_v[...] = jnp.broadcast_to(picked, (rows, LANES)).astype(jnp.int32)
    order_copy = pltpu.make_async_copy(order_v, order, order_sem)
    order_copy.start()

    local.wait()
    spread(p_ref, hf, tiles * thin)
    diagonals(1)

    fetch.wait()
    for k in range(slots):
        def spread_a(h, _, k=k):
            top = pl.multiple_of(h * 16, 16)
            base = pl.multiple_of((k * rows + h * 16) * tiles, 8)
            for t in range(tiles):
                tile = a_v[k, pl.ds(top, 16), t * LANES:(t + 1) * LANES].astype(F32)
                af[pl.ds(base + t * 8, 8), :] = tile[:8]
                af[pl.ds(base + (tiles + t) * 8, 8), :] = tile[8:]
            return 0
        lax.fori_loop(0, rows // 16, spread_a, 0)

    for copy, slot in zip(row_copies, (0, 2)):
        copy.wait()
        spread(halo_v.at[slot // 2], hf, slot * tiles * thin)
        diagonals(slot)

    cols_copy.wait()
    shift = (1 - g) * thin - z * thin

    def product(ih, _):
        for il in range(8):
            i = ih * 8 + il
            for k in range(slots):
                c = cols[k, i]
                place = jnp.clip(c - lax.div(c, rows) * (rows - thin) + shift, 0, 3 * thin - 1)
                left = af[pl.ds(k * rows * tiles + ih * 8 * tiles + il, tiles, stride=8), :].astype(BF)
                prod = jnp.dot(left, bd[place], preferred_element_type=F32)
                wv[i, :, k * LANES:(k + 1) * LANES] = jnp.concatenate(
                    [prod, pltpu.roll(prod, bs, 1)], axis=0).astype(BF)
        return 0
    lax.fori_loop(0, rows // 8, product, 0)

    def lefts(source, j):
        spread(source, pf, 0)
        for r in range(thin):
            packed = pf[pl.ds(r, tiles, stride=thin), :]
            stacked = jnp.concatenate([packed, pltpu.roll(packed, bs, 1)], axis=0).astype(BF)
            lv[j * thin + r] = lax.dot_general(
                pick, stacked, (((1,), (1,)), ((), ())), preferred_element_type=F32).astype(BF)

    lefts(p_ref, z)
    for d, copy in enumerate(col_copies, 1):
        copy.wait()
        lefts(own_v.at[d], lax.rem(z + ncol - d, ncol))

    order_copy.wait()

    def terms(j):
        i = jnp.clip(order[j, 0], 0, rows - 1)
        full = jnp.dot(lv[i], wv[i], preferred_element_type=F32)
        for k in range(slots):
            part = full[:, k * LANES:(k + 1) * LANES]
            yield k, jnp.where(low, part[:tiles], pltpu.roll(part[tiles:], bs, 1)).astype(BF)

    pair_copies = []
    for c in range(chunks):
        for j in range(c * CHUNK, (c + 1) * CHUNK):
            for k, term in terms(j):
                send_v[j, k] = term
        copy = pltpu.make_async_remote_copy(
            src_ref=send_v.at[pl.ds(c * CHUNK, CHUNK)], dst_ref=recv_v.at[pl.ds(c * CHUNK, CHUNK)],
            send_sem=pair_send.at[c], recv_sem=pair_recv.at[c], device_id={"row": pair}, device_id_type=MESH)
        copy.start()
        pair_copies.append(copy)
    for c in range(chunks):
        pair_copies[c].wait_recv()
        for j in range(c * CHUNK, (c + 1) * CHUNK):
            for k, term in terms(half + j):
                total = term.astype(F32) + recv_v[j, k].astype(F32)
                of[pl.ds((k * half + j // 8 * 8) * tiles + j % 8, tiles, stride=8), :] = total
    for k in range(slots):
        for h in range(half // 16):
            base = (k * half + h * 16) * tiles
            for t in range(tiles):
                tile = jnp.concatenate(
                    [of[pl.ds(base + t * 8, 8), :], of[pl.ds(base + (tiles + t) * 8, 8), :]], axis=0)
                out_ref[k, h * 16:(h + 1) * 16, t * LANES:(t + 1) * LANES] = tile.astype(BF)
    for copy in pair_copies:
        copy.wait_send()


def on_device(nrow, ncol, a_blocks, columns, prolong, partner):
    rows, slots, size = a_blocks.shape
    thin = prolong.shape[0]
    bs = math.isqrt(size)
    tiles = size // LANES
    half = rows // 2
    chunks = half // CHUNK
    dims = (nrow, ncol, rows, slots, thin, size, bs)
    hbm = pl.BlockSpec(memory_space=pltpu.HBM)
    vmem = pl.BlockSpec(memory_space=pltpu.VMEM)
    out = pl.pallas_call(
        functools.partial(kernel, dims),
        out_shape=pltpu.VMEM((slots, half, size), BF),
        in_specs=[hbm] * 4,
        out_specs=vmem,
        scratch_shapes=[
            pltpu.VMEM((1, rows), jnp.int32),
            pltpu.VMEM((rows, LANES), jnp.int32),
            pltpu.SMEM((rows, LANES), jnp.int32),
            pltpu.SMEM((slots, rows), jnp.int32),
            pltpu.VMEM((thin, size), BF),
            pltpu.VMEM((slots, rows, size), BF),
            pltpu.VMEM((ncol, thin, size), BF),
            pltpu.VMEM((2, thin, size), BF),
            pltpu.VMEM((slots * rows * tiles, LANES), F32),
            pltpu.VMEM((3 * tiles * thin, LANES), F32),
            pltpu.VMEM((slots * half * tiles, LANES), F32),
            pltpu.VMEM((tiles * thin, LANES), F32),
            pltpu.VMEM((3 * thin, LANES, LANES), BF),
            pltpu.VMEM((rows, bs, bs), BF),
            pltpu.VMEM((rows, bs, slots * LANES), BF),
            pltpu.VMEM((half, slots, tiles, LANES), BF),
            pltpu.VMEM((half, slots, tiles, LANES), BF),
            pltpu.SemaphoreType.DMA,
            pltpu.SemaphoreType.DMA,
            pltpu.SemaphoreType.DMA,
            pltpu.SemaphoreType.DMA,
            pltpu.SemaphoreType.DMA,
            pltpu.SemaphoreType.DMA((2,)),
            pltpu.SemaphoreType.DMA((2,)),
            pltpu.SemaphoreType.DMA((ncol,)),
            pltpu.SemaphoreType.DMA((ncol,)),
            pltpu.SemaphoreType.DMA((chunks,)),
            pltpu.SemaphoreType.DMA((chunks,)),
        ],
        compiler_params=pltpu.CompilerParams(
            collective_id=0, has_side_effects=True, vmem_limit_bytes=32 * 2**20),
    )(*(pltpu.with_memory_space_constraint(x, pltpu.HBM) for x in (partner.reshape(1, rows), columns.T, prolong, a_blocks.transpose(1, 0, 2))))
    return out.transpose(1, 0, 2)


def solution(mesh):
    in_specs = (P("row", "col", None), P("row", "col"), P(("row", "col"), None), P("row"))
    out_specs = P("row", "col", None)
    return jax.shard_map(
        functools.partial(on_device, mesh.shape["row"], mesh.shape["col"]),
        mesh=mesh, in_specs=in_specs, out_specs=out_specs, check_vma=False
    )
```

profile of v0, /device:TPU:1, one launch (start us, length us, event | category | flops | bytes accessed | tf_op | source)
XLA Modules:
  0.0 15.3 jit_solution(7906315486231092552)
XLA Ops:
  0.0 14.5 %shard_map.46 = bf16[3,16,4096]{2,1,0:T(8,128)(2,1)S(1)} custom-call(s32[1,32]{1,0:T(1,128)} %bitcast.7, s32[3,32]{1,0:T(4,128)} %bitcast.6, bf16[8,4096]{1,0:T(8,128)(2,1)} %p_hbm.1, bf16[3,32,4096]{2,1,0:T(8,128)(2,1)} %bitcast.5), custom_call_target="tpu_custom_call" | custom-call | tf_op jit(solution)/shard_map/pallas_call | solution.py:200
  14.5 0.7 %copy.6 = bf16[16,3,4096]{2,0,1:T(8,128)(2,1)} copy(bf16[16,3,4096]{2,0,1:T(8,128)(2,1)S(1)} %bitcast.4) | data formatting | bytes 786432
where the time goes:
time: 15.4 us; the launch traced here: 15.3 us
  Pallas kernels  14.5 us (94%)
  local copies, waits for them, and re-layouts  0.75 us (5%)
    pallas_call x1, Pallas kernels, on_device(): pl.pallas_call(functools.partial(kernel, dims), out_shape=pltpu.VMEM((slo...  14.5 us
    unnamed x1, local copies, waits for them, and re-layouts  0.75 us

commit v1 on v0

v1 whole, which is shorter than its diff:
```python
import functools
import math

import jax
import jax.numpy as jnp
from jax import lax
from jax.experimental import pallas as pl
from jax.experimental.pallas import tpu as pltpu
from jax.sharding import PartitionSpec as P

MESH = pl.DeviceIdType.MESH
BF = jnp.bfloat16
F32 = jnp.float32
LANES = 128


def iota(shape, dim):
    return lax.broadcasted_iota(jnp.int32, shape, dim)


def onehot(mask):
    return jnp.where(mask, 1.0, 0.0).astype(BF)


def kernel(dims, partner_hbm, cols_hbm, p_hbm, a_hbm, out_ref, partner_v, order_v, order, cols, p_ref, a_v, own_v, halo_v, af, hf, of, pf, bd, lv, wv, term_v, recv_v,
           partner_sem, order_sem, cols_sem, p_sem, a_sem, row_ready, col_ready, row_send, row_recv, col_send, col_recv, pair_send, pair_recv):
    nrow, ncol, rows, slots, thin, size, bs = dims
    tiles = size // LANES
    half = rows // 2
    g = lax.axis_index("row")
    z = lax.axis_index("col")
    odd = lax.rem(g, 2)
    pair = g + 1 - 2 * odd

    barrier = pltpu.get_barrier_semaphore()
    for d in range(ncol - 1, 0, -1):
        @pl.when(z + d < ncol)
        def _(d=d):
            pl.semaphore_signal(barrier, inc=1, device_id={"col": z + d}, device_id_type=MESH)

    @pl.when(g + 1 < nrow)
    def _():
        pl.semaphore_signal(barrier, inc=1, device_id={"row": g + 1}, device_id_type=MESH)

    local = pltpu.make_async_copy(p_hbm, p_ref, p_sem)
    local.start()
    partner_copy = pltpu.make_async_copy(partner_hbm, partner_v, partner_sem)
    partner_copy.start()
    cols_copy = pltpu.make_async_copy(cols_hbm, cols, cols_sem)
    cols_copy.start()
    fetch = pltpu.make_async_copy(a_hbm, a_v, a_sem)
    fetch.start()
    greeted = z + jnp.minimum(g, 1)

    @pl.when(greeted > 0)
    def _():
        pl.semaphore_wait(barrier, greeted)

    def col_copy(target, source):
        return pltpu.make_async_remote_copy(
            src_ref=p_hbm, dst_ref=own_v.at[source], send_sem=col_send.at[target], recv_sem=col_recv.at[source],
            device_id={"col": target}, device_id_type=MESH)

    def row_copy(target, slot):
        return pltpu.make_async_remote_copy(
            src_ref=p_hbm, dst_ref=halo_v.at[slot], send_sem=row_send.at[slot], recv_sem=row_recv.at[slot],
            device_id={"row": target}, device_id_type=MESH)

    def pair_copy(source):
        place = pl.ds(source * thin, thin)
        return pltpu.make_async_remote_copy(
            src_ref=term_v.at[place], dst_ref=recv_v.at[place],
            send_sem=pair_send.at[source], recv_sem=pair_recv.at[source], device_id={"row": pair}, device_id_type=MESH)

    def send_down(target):
        @pl.when(target < z)
        def _():
            col_copy(target, z).start()

    send_down(0)

    @pl.when(g > 0)
    def _():
        row_copy(g - 1, 1).start()
        pl.semaphore_signal(row_ready, inc=1, device_id={"row": g - 1}, device_id_type=MESH)

    for d in range(1, ncol):
        @pl.when(z >= d)
        def _(d=d):
            pl.semaphore_signal(col_ready.at[d], inc=1, device_id={"col": z - d}, device_id_type=MESH)

    def send_up(d):
        @pl.when(z + d < ncol)
        def _():
            pl.semaphore_wait(col_ready.at[d], 1)
            col_copy(z + d, z).start()

    def spread(source, target, base):
        for t in range(tiles):
            target[pl.ds(base + t * thin, thin), :] = source[:, t * LANES:(t + 1) * LANES].astype(F32)

    low = iota((tiles, LANES), 1) < bs
    r2, c2 = iota((2 * bs, 2 * bs), 0), iota((2 * bs, 2 * bs), 1)
    rh, ch = r2 // bs, c2 // bs
    rm, cm = r2 - rh * bs, c2 - ch * bs
    cs = cm // tiles
    weave = onehot((rh == ch) & (2 * (cm - cs * tiles) + cs == rm))
    r1, c1 = iota((bs, LANES), 0), iota((bs, LANES), 1)
    s1 = r1 // tiles
    pick = onehot(c1 == 2 * (r1 - s1 * tiles) + s1)

    def diagonals(slot):
        base = slot * tiles * thin
        for r in range(thin):
            packed = hf[pl.ds(base + r, tiles, stride=thin), :]
            turned = pltpu.roll(packed, bs, 1)
            zero = jnp.zeros_like(packed)
            stacked = jnp.concatenate(
                [jnp.where(low, packed, zero), jnp.where(low, turned, zero),
                 jnp.where(low, zero, turned), jnp.where(low, zero, packed)], axis=0).astype(BF)
            bd[slot * thin + r] = jnp.dot(weave, stacked, preferred_element_type=F32).astype(BF)

    local.wait()
    spread(p_ref, hf, tiles * thin)
    diagonals(1)
    for target in range(1, ncol - 1):
        @pl.when(z == ncol - 1)
        def _(target=target):
            send_down(target)

    partner_copy.wait()
    place = iota((rows, rows), 0)
    entry = iota((rows, rows), 1)
    held = jnp.broadcast_to(partner_v[...], (rows, rows))
    matched = jnp.where(odd == 1, jnp.where(held == place, entry, 0), jnp.where(entry == place, held, 0))
    picked = jnp.sum(matched.astype(F32), axis=1, keepdims=True)
    order_v[...] = jnp.broadcast_to(picked, (rows, LANES)).astype(jnp.int32)
    order_copy = pltpu.make_async_copy(order_v, order, order_sem)
    order_copy.start()

    @pl.when(g + 1 < nrow)
    def _():
        pl.semaphore_wait(row_ready, 1)
        row_copy(g + 1, 0).start()

    fetch.wait()
    for k in range(slots):
        def spread_a(h, _, k=k):
            top = pl.multiple_of(h * 16, 16)
            base = pl.multiple_of((k * rows + h * 16) * tiles, 8)
            for t in range(tiles):
                tile = a_v[k, pl.ds(top, 16), t * LANES:(t + 1) * LANES].astype(F32)
                af[pl.ds(base + t * 8, 8), :] = tile[:8]
                af[pl.ds(base + (tiles + t) * 8, 8), :] = tile[8:]
            return 0
        lax.fori_loop(0, rows // 16, spread_a, 0)

    send_up(1)

    def halo(slot):
        row_copy(pair, slot).wait_recv()
        spread(halo_v.at[slot], hf, 2 * slot * tiles * thin)
        diagonals(2 * slot)

    @pl.when(g + 1 < nrow)
    def _():
        halo(1)
    for target in range(1, ncol - 1):
        @pl.when(z < ncol - 1)
        def _(target=target):
            send_down(target)
    for d in range(2, ncol):
        send_up(d)

    @pl.when(g > 0)
    def _():
        halo(0)

    cols_copy.wait()
    shift = (1 - g) * thin - z * thin

    def product(ih, _):
        for il in range(8):
            i = ih * 8 + il
            for k in range(slots):
                c = cols[k, i]
                place = jnp.clip(c - lax.div(c, rows) * (rows - thin) + shift, 0, 3 * thin - 1)
                left = af[pl.ds(k * rows * tiles + ih * 8 * tiles + il, tiles, stride=8), :].astype(BF)
                prod = jnp.dot(left, bd[place], preferred_element_type=F32)
                wv[i, :, k * LANES:(k + 1) * LANES] = jnp.concatenate(
                    [prod, pltpu.roll(prod, bs, 1)], axis=0).astype(BF)
        return 0
    lax.fori_loop(0, rows // 8, product, 0)

    def lefts(source, j):
        spread(source, pf, 0)
        for r in range(thin):
            packed = pf[pl.ds(r, tiles, stride=thin), :]
            stacked = jnp.concatenate([packed, pltpu.roll(packed, bs, 1)], axis=0).astype(BF)
            lv[j * thin + r] = lax.dot_general(
                pick, stacked, (((1,), (1,)), ((), ())), preferred_element_type=F32).astype(BF)

    def terms(source, j):
        lefts(source, j)
        for r in range(thin):
            i = j * thin + r
            full = jnp.dot(lv[i], wv[i], preferred_element_type=F32)
            for k in range(slots):
                part = full[:, k * LANES:(k + 1) * LANES]
                term_v[i, k] = jnp.where(low, part[:tiles], pltpu.roll(part[tiles:], bs, 1)).astype(BF)

        @pl.when((odd == 1) | (2 * j >= ncol))
        def _():
            pair_copy(j).start()

    inner = jnp.minimum(z, ncol - 1 - z)
    terms(p_ref, z)
    for s in range(1, ncol):
        near = z - (s + 1) // 2 if s % 2 else z + s // 2
        j = jnp.where(s <= 2 * inner, near, jnp.where(2 * z < ncol - 1, s, ncol - 1 - s))
        col_copy(j, j).wait_recv()
        terms(own_v.at[j], j)

    order_copy.wait()
    for j in range(ncol):
        @pl.when((odd == 0) | (2 * j >= ncol))
        def _(j=j):
            pair_copy(j).wait_recv()
    for j in range(half):
        found = jnp.clip(order[odd * half + j, 0], 0, rows - 1)
        mine = jnp.where(odd == 1, found, j)
        other = jnp.where(odd == 1, half + j, found)
        for k in range(slots):
            total = term_v[mine, k].astype(F32) + recv_v[other, k].astype(F32)
            of[pl.ds((k * half + j // 8 * 8) * tiles + j % 8, tiles, stride=8), :] = total
    for k in range(slots):
        for h in range(half // 16):
            base = (k * half + h * 16) * tiles
            for t in range(tiles):
                tile = jnp.concatenate(
                    [of[pl.ds(base + t * 8, 8), :], of[pl.ds(base + (tiles + t) * 8, 8), :]], axis=0)
                out_ref[k, h * 16:(h + 1) * 16, t * LANES:(t + 1) * LANES] = tile.astype(BF)

    for j in range(ncol):
        @pl.when((odd == 1) | (2 * j >= ncol))
        def _(j=j):
            pair_copy(j).wait_send()

        @pl.when(j != z)
        def _(j=j):
            col_copy(j, z).wait_send()
    for slot in range(2):
        @pl.when((g > 0) if slot else (g + 1 < nrow))
        def _(slot=slot):
            row_copy(pair, slot).wait_send()


def on_device(nrow, ncol, a_blocks, columns, prolong, partner):
    rows, slots, size = a_blocks.shape
    thin = prolong.shape[0]
    bs = math.isqrt(size)
    tiles = size // LANES
    half = rows // 2
    dims = (nrow, ncol, rows, slots, thin, size, bs)
    hbm = pl.BlockSpec(memory_space=pltpu.HBM)
    vmem = pl.BlockSpec(memory_space=pltpu.VMEM)
    out = pl.pallas_call(
        functools.partial(kernel, dims),
        out_shape=pltpu.VMEM((slots, half, size), BF),
        in_specs=[hbm] * 4,
        out_specs=vmem,
        scratch_shapes=[
            pltpu.VMEM((1, rows), jnp.int32),
            pltpu.VMEM((rows, LANES), jnp.int32),
            pltpu.SMEM((rows, LANES), jnp.int32),
            pltpu.SMEM((slots, rows), jnp.int32),
            pltpu.VMEM((thin, size), BF),
            pltpu.VMEM((slots, rows, size), BF),
            pltpu.VMEM((ncol, thin, size), BF),
            pltpu.VMEM((2, thin, size), BF),
            pltpu.VMEM((slots * rows * tiles, LANES), F32),
            pltpu.VMEM((3 * tiles * thin, LANES), F32),
            pltpu.VMEM((slots * half * tiles, LANES), F32),
            pltpu.VMEM((tiles * thin, LANES), F32),
            pltpu.VMEM((3 * thin, LANES, LANES), BF),
            pltpu.VMEM((rows, bs, bs), BF),
            pltpu.VMEM((rows, bs, slots * LANES), BF),
            pltpu.VMEM((rows, slots, tiles, LANES), BF),
            pltpu.VMEM((rows, slots, tiles, LANES), BF),
            pltpu.SemaphoreType.DMA,
            pltpu.SemaphoreType.DMA,
            pltpu.SemaphoreType.DMA,
            pltpu.SemaphoreType.DMA,
            pltpu.SemaphoreType.DMA,
            pltpu.SemaphoreType.REGULAR,
            pltpu.SemaphoreType.REGULAR((ncol,)),
            pltpu.SemaphoreType.DMA((2,)),
            pltpu.SemaphoreType.DMA((2,)),
            pltpu.SemaphoreType.DMA((ncol,)),
            pltpu.SemaphoreType.DMA((ncol,)),
            pltpu.SemaphoreType.DMA((ncol,)),
            pltpu.SemaphoreType.DMA((ncol,)),
        ],
        compiler_params=pltpu.CompilerParams(
            collective_id=0, has_side_effects=True, vmem_limit_bytes=32 * 2**20),
    )(*(pltpu.with_memory_space_constraint(x, pltpu.HBM) for x in (partner.reshape(1, rows), columns.T, prolong, a_blocks.transpose(1, 0, 2))))
    return out.transpose(1, 0, 2)


def solution(mesh):
    in_specs = (P("row", "col", None), P("row", "col"), P(("row", "col"), None), P("row"))
    out_specs = P("row", "col", None)
    return jax.shard_map(
        functools.partial(on_device, mesh.shape["row"], mesh.shape["col"]),
        mesh=mesh, in_specs=in_specs, out_specs=out_specs, check_vma=False
    )
```

time: 15.4 us -> 13.2 us (0.86)
  Pallas kernels: 14.5 us -> 12.2 us
    pallas_call x1, Pallas kernels: 14.5 us -> 12.2 us  [on_device(): pl.pallas_call(functools.partial(kernel, dims), out_shape=pltpu.VMEM((slo...]
where the time goes in v1:
time: 13.2 us; the launch traced here: 13 us
  Pallas kernels  12.2 us (92%)
  local copies, waits for them, and re-layouts  0.75 us (6%)
    pallas_call x1, Pallas kernels, on_device(): pl.pallas_call(functools.partial(kernel, dims), out_shape=pltpu.VMEM((slo...  12.2 us
    unnamed x1, local copies, waits for them, and re-layouts  0.75 us

profile of v1, /device:TPU:1, one launch (start us, length us, event | category | flops | bytes accessed | tf_op | source)
XLA Modules:
  0.0 13.0 jit_solution(11848634423618297217)
XLA Ops:
  0.0 12.2 %shard_map.46 = bf16[3,16,4096]{2,1,0:T(8,128)(2,1)S(1)} custom-call(s32[1,32]{1,0:T(1,128)} %bitcast.7, s32[3,32]{1,0:T(4,128)} %bitcast.6, bf16[8,4096]{1,0:T(8,128)(2,1)} %p_hbm.1, bf16[3,32,4096]{2,1,0:T(8,128)(2,1)} %bitcast.5), custom_call_target="tpu_custom_call" | custom-call | tf_op jit(solution)/shard_map/pallas_call | solution.py:267
  12.2 0.7 %copy.6 = bf16[16,3,4096]{2,0,1:T(8,128)(2,1)} copy(bf16[16,3,4096]{2,0,1:T(8,128)(2,1)S(1)} %bitcast.4) | data formatting | bytes 786432

commit v2 on v1

--- a/solution.py
+++ b/solution.py
@@ -107,7 +107,7 @@
     weave = onehot((rh == ch) & (2 * (cm - cs * tiles) + cs == rm))
     r1, c1 = iota((bs, LANES), 0), iota((bs, LANES), 1)
     s1 = r1 // tiles
-    pick = onehot(c1 == 2 * (r1 - s1 * tiles) + s1)
+    pick = onehot(c1 == 2 * (r1 - s1 * tiles) + s1 * (bs + 1))
 
     def diagonals(slot):
         base = slot * tiles * thin
@@ -123,10 +123,6 @@
     local.wait()
     spread(p_ref, hf, tiles * thin)
     diagonals(1)
-    for target in range(1, ncol - 1):
-        @pl.when(z == ncol - 1)
-        def _(target=target):
-            send_down(target)
 
     partner_copy.wait()
     place = iota((rows, rows), 0)
@@ -138,11 +134,13 @@
     order_copy = pltpu.make_async_copy(order_v, order, order_sem)
     order_copy.start()
 
-    @pl.when(g + 1 < nrow)
-    def _():
-        pl.semaphore_wait(row_ready, 1)
-        row_copy(g + 1, 0).start()
-
+    def greet_row(side):
+        @pl.when((g + 1 < nrow) & (odd == side))
+        def _():
+            pl.semaphore_wait(row_ready, 1)
+            row_copy(g + 1, 0).start()
+
+    greet_row(0)
     fetch.wait()
     for k in range(slots):
         def spread_a(h, _, k=k):
@@ -156,6 +154,9 @@
         lax.fori_loop(0, rows // 16, spread_a, 0)
 
     send_up(1)
+    greet_row(1)
+    for d in range(2, ncol):
+        send_up(d)
 
     def halo(slot):
         row_copy(pair, slot).wait_recv()
@@ -166,11 +167,7 @@
     def _():
         halo(1)
     for target in range(1, ncol - 1):
-        @pl.when(z < ncol - 1)
-        def _(target=target):
-            send_down(target)
-    for d in range(2, ncol):
-        send_up(d)
+        send_down(target)
 
     @pl.when(g > 0)
     def _():
@@ -207,7 +204,7 @@
             full = jnp.dot(lv[i], wv[i], preferred_element_type=F32)
             for k in range(slots):
                 part = full[:, k * LANES:(k + 1) * LANES]
-                term_v[i, k] = jnp.where(low, part[:tiles], pltpu.roll(part[tiles:], bs, 1)).astype(BF)
+                term_v[i, k] = jnp.where(low, part[:tiles], part[tiles:]).astype(BF)
 
         @pl.when((odd == 1) | (2 * j >= ncol))
         def _():

time: 13.2 us -> 12.8 us (0.970)
  the two profiles are of different devices: /device:TPU:1 before, /device:TPU:15 now
where the time goes in v2:
time: 12.8 us; the launch traced here: 12.7 us
  Pallas kernels  11.9 us (93%)
  local copies, waits for them, and re-layouts  0.75 us (6%)
    pallas_call x1, Pallas kernels, on_device(): pl.pallas_call(functools.partial(kernel, dims), out_shape=pltpu.VMEM((slo...  11.9 us
    unnamed x1, local copies, waits for them, and re-layouts  0.75 us

profile of v2, /device:TPU:15, one launch (start us, length us, event | category | flops | bytes accessed | tf_op | source)
XLA Modules:
  0.0 12.7 jit_solution(15078011845656544068)
XLA Ops:
  0.0 11.9 %shard_map.46 = bf16[3,16,4096]{2,1,0:T(8,128)(2,1)S(1)} custom-call(s32[1,32]{1,0:T(1,128)} %bitcast.7, s32[3,32]{1,0:T(4,128)} %bitcast.6, bf16[8,4096]{1,0:T(8,128)(2,1)} %p_hbm.1, bf16[3,32,4096]{2,1,0:T(8,128)(2,1)} %bitcast.5), custom_call_target="tpu_custom_call" | custom-call | tf_op jit(solution)/shard_map/pallas_call | solution.py:264
  11.9 0.7 %copy.6 = bf16[16,3,4096]{2,0,1:T(8,128)(2,1)} copy(bf16[16,3,4096]{2,0,1:T(8,128)(2,1)S(1)} %bitcast.4) | data formatting | bytes 786432
